TPU v7x, 32 devices: a whole 2x2x4 slice. The times are simulated.
32 devices in a mesh: grp: 2 (over y), dev: 16 (over z, x, core).
Axes of the slice: x: 2, y: 2, z: 4, core: 2. Of those that a mesh axis runs over, the one named last changes fastest.
Arguments:
- sources: bfloat16 [65536, 768], P(('grp', 'dev')), may hold values from -6 to 6
- encoder: bfloat16 [65536, 256], P(('grp', 'dev')), may hold values from -0.125 to 0.125
- section_weight: bfloat16 [32, 4, 2, 256, 256], P(('grp', 'dev')), may hold values from -0.25 to 0.25
- cross_weight: bfloat16 [2, 16, 2, 256, 256], P('grp', 'dev'), may hold values from -0.25 to 0.25
- local_weight: bfloat16 [32, 14, 256, 256], P(('grp', 'dev')), may hold values from -0.375 to 0.375
- decoder: bfloat16 [65536, 256], P(('grp', 'dev')), may hold values from -0.375 to 0.375
Outputs:
- target_values: bfloat16 [65536, 768], P(('grp', 'dev'))
All inputs are finite; a program needn't handle non-finite values.
Results may differ from a plain program's by a relative error of at most 0.02.
Values may be sent and summed in bfloat16 or wider, within the bound.
No kernel may reach another device: no remote copies, remote signals or barrier semaphores. Data moves between devices by JAX's collectives and lax.ppermute only.
A program may use at most 64 MiB of HBM per device.

v0:
```python
import jax
import jax.numpy as jnp
from jax import lax
from jax.sharding import PartitionSpec as P

K = 256
LOCAL = 3


def from_partner(block, axis, bit):
    count = lax.axis_size(axis)
    route = []
    for low in range(count):
        high = low | 1 << bit
        if high != low and high < count:
            route += [(low, high), (high, low)]
    return lax.ppermute(block, axis, route)


def shards(sources, encoder, section_weight, cross_weight, local_weight, decoder):
    coeffs = lax.dot_general(
        encoder, sources, (((0,), (0,)), ((), ())), preferred_element_type=jnp.float32
    ).astype(jnp.bfloat16)
    section_count = lax.axis_size("dev").bit_length() - 1
    for section_bit in range(section_count):
        partner = from_partner(coeffs, "dev", section_bit)
        keep_matrix = section_weight[0, section_bit, 0]
        take_matrix = section_weight[0, section_bit, 1]
        coeffs = (
            jnp.dot(keep_matrix, coeffs, preferred_element_type=jnp.float32)
            + jnp.dot(take_matrix, partner, preferred_element_type=jnp.float32)
        ).astype(jnp.bfloat16)
    own_cross = cross_weight[0, 0]
    merged = jnp.einsum(
        "hkl,hlr->kr",
        own_cross,
        lax.all_gather(coeffs[None], "grp", axis=0, tiled=True),
        preferred_element_type=jnp.float32,
    ).astype(jnp.bfloat16)
    blocks = merged[None]
    offset = 0
    for depth_level in range(LOCAL):
        children = 2 ** (depth_level + 1)
        matrices = local_weight[0, offset : offset + children].reshape(children // 2, 2, K, K)
        blocks = jnp.einsum("jckl,jlr->jckr", matrices, blocks, preferred_element_type=jnp.float32)
        blocks = blocks.reshape(children, K, blocks.shape[-1]).astype(jnp.bfloat16)
        offset = offset + children
    decoder_leaves = decoder.reshape(2**LOCAL, -1, K)
    target_values = jnp.einsum(
        "ctk,ckr->ctr", decoder_leaves, blocks, preferred_element_type=jnp.float32
    )
    return target_values.reshape(-1, blocks.shape[-1]).astype(jnp.bfloat16)


def solution(mesh):
    placed = (
        P(("grp", "dev"), None),
        P(("grp", "dev"), None),
        P(("grp", "dev"), None, None, None, None),
        P("grp", "dev", None, None, None),
        P(("grp", "dev"), None, None, None),
        P(("grp", "dev"), None),
    )
    return jax.shard_map(
        shards, mesh=mesh, in_specs=placed, out_specs=P(("grp", "dev"), None), check_vma=False
    )
```

profile of v0, /device:TPU:0, one launch (start us, length us, event | category | flops | bytes accessed | tf_op | source)
XLA Modules:
  0.0 69.3 jit_solution(10886615628694809823)
XLA Ops:
  0.0 1.9 %copy-done = bf16[2048,768]{1,0:T(8,128)(2,1)S(1)} copy-done((bf16[2048,768]{1,0:T(8,128)(2,1)S(1)}, bf16[2048,768]{1,0:T(8,128)(2,1)}, u32[]{:S(2)}) %copy-start) | copy-done | bytes 3145752
  1.9 2.2 %convolution_convert_fusion.4 = bf16[256,768]{1,0:T(8,128)(2,1)S(1)} fusion(bf16[2048,256]{1,0:T(8,128)(2,1)} %param.7, bf16[2048,768]{1,0:T(8,128)(2,1)S(1)} %copy-done), kind=kOutput, calls=%fused_computation.15 | convolution fusion | flops 805502976 | bytes 4587520 | tf_op jit(solution)/shard_map/dot_general | solution.py:21
  4.1 0.6 collective-permute-start
  4.7 0.3 fusion.25
  5.0 1.0 %collective-permute-done = bf16[256,768]{1,0:T(8,128)(2,1)S(1)} collective-permute-done((bf16[256,768]{1,0:T(8,128)(2,1)S(1)}, bf16[256,768]{1,0:T(8,128)(2,1)S(1)}, u32[]{:S(2)}, u32[]{:S(2)}) %collective-permute-start) | collective-permute-done | bytes 393248 | tf_op jit(solution)/shard_map/ppermute | solution.py:17
  6.0 0.3 fusion.1
  6.4 2.9 %collective-permute-start.1 = (bf16[256,768]{0,1:T(8,128)(2,1)S(1)}, bf16[256,768]{0,1:T(8,128)(2,1)S(1)}, u32[]{:S(2)}, u32[]{:S(2)}) collective-permute-start(bf16[256,768]{0,1:T(8,128)(2,1)S(1)} %bitcast.93), channel_id=1, source_target_pairs={{0,2},{2,0},{1,3},{3,1},{4,6},{6,4},{5,7},{7,5},{8,10},{10,8},{9,1... | collective-permute-start | bytes 1179656 | tf_op jit(solution)/shard_map/ppermute | solution.py:17
  9.3 0.3 fusion.22
  9.6 9.1 %collective-permute-done.1 = bf16[256,768]{0,1:T(8,128)(2,1)S(1)} collective-permute-done((bf16[256,768]{0,1:T(8,128)(2,1)S(1)}, bf16[256,768]{0,1:T(8,128)(2,1)S(1)}, u32[]{:S(2)}, u32[]{:S(2)}) %collective-permute-start.1) | collective-permute-done | bytes 393248 | tf_op jit(solution)/shard_map/ppermute | solution.py:17
  18.7 0.3 fusion.2
  19.0 1.9 %collective-permute-start.2 = (bf16[256,768]{0,1:T(8,128)(2,1)S(1)}, bf16[256,768]{0,1:T(8,128)(2,1)S(1)}, u32[]{:S(2)}, u32[]{:S(2)}) collective-permute-start(bf16[256,768]{0,1:T(8,128)(2,1)S(1)} %bitcast.94), channel_id=1, source_target_pairs={{0,4},{4,0},{1,5},{5,1},{2,6},{6,2},{3,7},{7,3},{8,12},{12,8},{9,1... | collective-permute-start | bytes 1179656 | tf_op jit(solution)/shard_map/ppermute | solution.py:17
  21.2 8.5 %collective-permute-done.2 = bf16[256,768]{0,1:T(8,128)(2,1)S(1)} collective-permute-done((bf16[256,768]{0,1:T(8,128)(2,1)S(1)}, bf16[256,768]{0,1:T(8,128)(2,1)S(1)}, u32[]{:S(2)}, u32[]{:S(2)}) %collective-permute-start.2) | collective-permute-done | bytes 393248 | tf_op jit(solution)/shard_map/ppermute | solution.py:17
  29.6 0.3 fusion.3
  29.9 2.6 %collective-permute-start.3 = (bf16[256,768]{0,1:T(8,128)(2,1)S(1)}, bf16[256,768]{0,1:T(8,128)(2,1)S(1)}, u32[]{:S(2)}, u32[]{:S(2)}) collective-permute-start(bf16[256,768]{0,1:T(8,128)(2,1)S(1)} %bitcast.92), channel_id=1, source_target_pairs={{0,8},{8,0},{1,9},{9,1},{2,10},{10,2},{3,11},{11,3},{4,12},{12,4},... | collective-permute-start | bytes 1179656 | tf_op jit(solution)/shard_map/ppermute | solution.py:17
  32.6 0.8 %slice.42 = bf16[1,4,256,256]{3,2,1,0:T(8,128)(2,1)} slice(bf16[1,14,256,256]{3,2,1,0:T(8,128)(2,1)S(1)} %copy-done.1), slice={[0:1], [2:6], [0:256], [0:256]} | slice | bytes 1048576 | tf_op jit(solution)/shard_map/slice | solution.py:44
  33.4 1.0 %slice.43 = bf16[1,8,256,256]{3,2,1,0:T(8,128)(2,1)} slice(bf16[1,14,256,256]{3,2,1,0:T(8,128)(2,1)S(1)} %copy-done.1), slice={[0:1], [6:14], [0:256], [0:256]} | slice | bytes 2097152 | tf_op jit(solution)/shard_map/slice | solution.py:44
  34.4 0.3 fusion.16
  34.7 14.3 %collective-permute-done.3 = bf16[256,768]{0,1:T(8,128)(2,1)S(1)} collective-permute-done((bf16[256,768]{0,1:T(8,128)(2,1)S(1)}, bf16[256,768]{0,1:T(8,128)(2,1)S(1)}, u32[]{:S(2)}, u32[]{:S(2)}) %collective-permute-start.3) | collective-permute-done | bytes 393248 | tf_op jit(solution)/shard_map/ppermute | solution.py:17
  49.1 0.3 fusion.6
  49.4 11.0 %all-gather = bf16[512,768]{0,1:T(8,128)(2,1)S(1)} all-gather(bf16[256,768]{0,1:T(8,128)(2,1)S(1)} %fusion.6), channel_id=2, replica_groups=mesh['grp'=2,'dev'=16] {'grp'}, dimensions={0}, use_global_device_ids=true | all-gather | bytes 1179648 | tf_op jit(solution)/shard_map/all_gather | solution.py:37
  60.4 0.4 fusion.7
  60.8 3.1 %convolution_convert_fusion.2 = bf16[2,768,2,256]{3,1,2,0:T(8,128)(2,1)} fusion(bf16[2,2,256,256]{3,2,1,0:T(8,128)(2,1)} %bitcast.91, bf16[768,256,1]{1,0,2:T(8,128)(2,1)S(1)} %fusion.7, bf16[1,14,256,256]{3,2,1,0:T(8,128)(2,1)} %param.10), kind=kOutput, calls=%fused_computation.2 | convolution fusion | flops 605159424 | bytes 2752512 | tf_op jit(solution)/shard_map/jckl,jlr->jckr/dot_general | solution.py:45
  63.8 2.8 %convolution_convert_fusion.1 = bf16[4,768,2,256]{3,1,2,0:T(8,128)(2,1)S(1)} fusion(bf16[4,256,768,1]{1,2,3,0:T(8,128)(2,1)} %bitcast.89, bf16[4,2,256,256]{3,2,1,0:T(8,128)(2,1)} %bitcast.90), kind=kOutput, calls=%fused_computation.1 | convolution fusion | flops 806879232 | bytes 5767168 | tf_op jit(solution)/shard_map/jckl,jlr->jckr/dot_general | solution.py:45
  66.7 2.7 %convolution_convert_fusion = bf16[8,768,256]{1,2,0:T(8,128)(2,1)} fusion(bf16[8,256,768]{1,2,0:T(8,128)(2,1)S(1)} %bitcast.88, bf16[8,256,256]{2,1,0:T(8,128)(2,1)S(1)} %bitcast.95), kind=kOutput, calls=%fused_computation | convolution fusion | flops 806879232 | bytes 7340032 | tf_op jit(solution)/shard_map/ctk,ckr->ctr/dot_general | solution.py:49
  (10 shorter events, 0.3 us)
Async XLA Ops:
  0.0 1.9 %copy-start = (bf16[2048,768]{1,0:T(8,128)(2,1)S(1)}, bf16[2048,768]{1,0:T(8,128)(2,1)}, u32[]{:S(2)}) copy-start(bf16[2048,768]{1,0:T(8,128)(2,1)} %param.6) | copy-start | bytes 9437188
  0.0 4.7 %copy-start.3 = (bf16[1,4,2,256,256]{4,3,2,1,0:T(8,128)(2,1)S(1)}, bf16[1,4,2,256,256]{4,3,2,1,0:T(8,128)(2,1)}, u32[]{:S(2)}) copy-start(bf16[1,4,2,256,256]{4,3,2,1,0:T(8,128)(2,1)} %param.8) | copy-start | bytes 3145732
  4.1 1.9 %collective-permute-start = (bf16[256,768]{1,0:T(8,128)(2,1)S(1)}, bf16[256,768]{1,0:T(8,128)(2,1)S(1)}, u32[]{:S(2)}, u32[]{:S(2)}) collective-permute-start(bf16[256,768]{1,0:T(8,128)(2,1)S(1)} %convolution_convert_fusion.4), channel_id=1, source_target_pairs={{0,1},{1,0},{2,3},{3,2},{4,5},{5,4},{6,7},{7,6},{8,9},{9,8},{10,11... | collective-permute-start | bytes 1179656 | tf_op jit(solution)/shard_map/ppermute | solution.py:17
  6.4 26.2 %copy-start.1 = (bf16[1,14,256,256]{3,2,1,0:T(8,128)(2,1)S(1)}, bf16[1,14,256,256]{3,2,1,0:T(8,128)(2,1)}, u32[]{:S(2)}) copy-start(bf16[1,14,256,256]{3,2,1,0:T(8,128)(2,1)} %param.10) | copy-start | bytes 5505028
  6.4 12.3 %collective-permute-start.1 = (bf16[256,768]{0,1:T(8,128)(2,1)S(1)}, bf16[256,768]{0,1:T(8,128)(2,1)S(1)}, u32[]{:S(2)}, u32[]{:S(2)}) collective-permute-start(bf16[256,768]{0,1:T(8,128)(2,1)S(1)} %bitcast.93), channel_id=1, source_target_pairs={{0,2},{2,0},{1,3},{3,1},{4,6},{6,4},{5,7},{7,5},{8,10},{10,8},{9,1... | collective-permute-start | bytes 1179656 | tf_op jit(solution)/shard_map/ppermute | solution.py:17
  19.0 10.7 %collective-permute-start.2 = (bf16[256,768]{0,1:T(8,128)(2,1)S(1)}, bf16[256,768]{0,1:T(8,128)(2,1)S(1)}, u32[]{:S(2)}, u32[]{:S(2)}) collective-permute-start(bf16[256,768]{0,1:T(8,128)(2,1)S(1)} %bitcast.94), channel_id=1, source_target_pairs={{0,4},{4,0},{1,5},{5,1},{2,6},{6,2},{3,7},{7,3},{8,12},{12,8},{9,1... | collective-permute-start | bytes 1179656 | tf_op jit(solution)/shard_map/ppermute | solution.py:17
  29.9 19.1 %collective-permute-start.3 = (bf16[256,768]{0,1:T(8,128)(2,1)S(1)}, bf16[256,768]{0,1:T(8,128)(2,1)S(1)}, u32[]{:S(2)}, u32[]{:S(2)}) collective-permute-start(bf16[256,768]{0,1:T(8,128)(2,1)S(1)} %bitcast.92), channel_id=1, source_target_pairs={{0,8},{8,0},{1,9},{9,1},{2,10},{10,2},{3,11},{11,3},{4,12},{12,4},... | collective-permute-start | bytes 1179656 | tf_op jit(solution)/shard_map/ppermute | solution.py:17
  33.4 27.0 %copy-start.4 = (bf16[1,1,2,256,256]{4,3,2,1,0:T(8,128)(2,1)S(1)}, bf16[1,1,2,256,256]{4,3,2,1,0:T(8,128)(2,1)}, u32[]{:S(2)}) copy-start(bf16[1,1,2,256,256]{4,3,2,1,0:T(8,128)(2,1)} %param.9) | copy-start | bytes 786436
  63.8 2.8 %copy-start.2 = (bf16[2048,256]{1,0:T(8,128)(2,1)S(1)}, bf16[2048,256]{1,0:T(8,128)(2,1)}, u32[]{:S(2)}) copy-start(bf16[2048,256]{1,0:T(8,128)(2,1)} %param.11) | copy-start | bytes 3145732
where the time goes:
time: 69.5 us; the launch traced here: 69.3 us
  waiting for transfers between devices  32.9 us (47%)
  matrix products  13.5 us (19%)
  blocking collectives  11 us (16%)
  starting transfers between devices  7.99 us (11%)
  local copies, waits for them, and re-layouts  3.79 us (5%)
    ppermute x4, waiting for transfers between devices, from_partner(): return lax.ppermute(block, axis, route)  32.9 us
    all_gather x1, blocking collectives, shards(): lax.all_gather(coeffs[None], 'grp', axis=0, tiled=True)  11 us
    ppermute x4, starting transfers between devices, from_partner(): return lax.ppermute(block, axis, route)  7.99 us
    dot_general x2, matrix products, shards(): jnp.einsum('jckl,jlr->jckr', matrices, blocks, preferred_element_type=jnp...  5.88 us
    dot_general x1, matrix products, shards(): jnp.einsum('ctk,ckr->ctr', decoder_leaves, blocks, preferred_element_type...  2.68 us
    dot_general x1, matrix products, shards(): lax.dot_general(encoder, sources, (((0,), (0,)), ((), ())), preferred_ele...  2.23 us
    unnamed x10, local copies, waits for them, and re-layouts  1.9 us
    slice x2, local copies, waits for them, and re-layouts, shards(): local_weight[0, offset:offset + children].reshape(children // 2, 2, K, K)  1.88 us
  transfers between devices with their start and end apart: 4, of which 4 were waited for; matrix products, arithmetic and copies ran while one was open for 4% of the time, Pallas kernels for 0%

commit v1 on v0

--- a/solution.py
+++ b/solution.py
@@ -5,6 +5,12 @@
 
 K = 256
 LOCAL = 3
+derive_panel = lambda sample, chip_axis, along_dim: jnp.concatenate(
+    lax.all_to_all(
+        jnp.stack([sample] * lax.psum(1, chip_axis), axis=0), chip_axis, split_axis=0, concat_axis=0
+    ),
+    along_dim,
+)
 
 
 def from_partner(block, axis, bit):
@@ -34,7 +40,7 @@
     merged = jnp.einsum(
         "hkl,hlr->kr",
         own_cross,
-        lax.all_gather(coeffs[None], "grp", axis=0, tiled=True),
+        derive_panel(coeffs[None], "grp", 0),
         preferred_element_type=jnp.float32,
     ).astype(jnp.bfloat16)
     blocks = merged[None]

time: 69.5 us -> 75.7 us (1.089)
  blocking collectives: 11 us -> 0 us
  waiting for transfers between devices: 32.9 us -> 41.3 us
  starting transfers between devices: 7.99 us -> 12.3 us
  local copies, waits for them, and re-layouts: 3.79 us -> 6.04 us
  matrix products: 13.5 us -> 14.7 us
  other arithmetic: 0 us -> 0.94 us
    all_gather x1 -> x0, blocking collectives: 11 us -> none  [shards(): lax.all_gather(coeffs[None], 'grp', axis=0, tiled=True)]
    all_to_all x0 -> x1, waiting for transfers between devices: none -> 6.47 us  [lax.all_to_all(jnp.stack([sample] * lax.psum(1, chip_axis), axis=0), chip...]
    all_to_all x0 -> x1, starting transfers between devices: none -> 4.33 us  [lax.all_to_all(jnp.stack([sample] * lax.psum(1, chip_axis), axis=0), chip...]
    slice x2, local copies, waits for them, and re-layouts: 1.88 us -> 4.14 us  [shards(): local_weight[0, offset:offset + children].reshape(children // 2, 2, K, K)]
    ppermute x4, waiting for transfers between devices: 32.9 us -> 34.8 us  [from_partner(): return lax.ppermute(block, axis, route)]
    dot_general x1, matrix products: 0.4 us -> 1.59 us  [shards(): jnp.einsum('hkl,hlr->kr', own_cross, derive_panel(coeffs[None], 'grp', 0)...]
    another operation x0 -> x1, other arithmetic: none -> 0.94 us  [jnp.stack([sample] * lax.psum(1, chip_axis), axis=0)]
    unnamed x10 -> x6, local copies, waits for them, and re-layouts: 1.9 us -> 1.89 us
  transfers between devices with their start and end apart: 4 -> 5, of which waited for: 4 -> 5; matrix products, arithmetic and copies ran while one was open for 4% -> 7% of each run, Pallas kernels for 0% -> 0%
where the time goes in v1:
time: 75.7 us; the launch traced here: 75.4 us
  waiting for transfers between devices  41.3 us (55%)
  matrix products  14.7 us (19%)
  starting transfers between devices  12.3 us (16%)
  local copies, waits for them, and re-layouts  6.04 us (8%)
  other arithmetic  0.94 us (1%)
    ppermute x4, waiting for transfers between devices, from_partner(): return lax.ppermute(block, axis, route)  34.8 us
    ppermute x4, starting transfers between devices, from_partner(): return lax.ppermute(block, axis, route)  7.98 us
    all_to_all x1, waiting for transfers between devices, lax.all_to_all(jnp.stack([sample] * lax.psum(1, chip_axis), axis=0), chip...  6.47 us
    dot_general x2, matrix products, shards(): jnp.einsum('jckl,jlr->jckr', matrices, blocks, preferred_element_type=jnp...  5.88 us
    all_to_all x1, starting transfers between devices, lax.all_to_all(jnp.stack([sample] * lax.psum(1, chip_axis), axis=0), chip...  4.33 us
    slice x2, local copies, waits for them, and re-layouts, shards(): local_weight[0, offset:offset + children].reshape(children // 2, 2, K, K)  4.14 us
    dot_general x1, matrix products, shards(): jnp.einsum('ctk,ckr->ctr', decoder_leaves, blocks, preferred_element_type...  2.68 us
    dot_general x1, matrix products, shards(): lax.dot_general(encoder, sources, (((0,), (0,)), ((), ())), preferred_ele...  2.23 us
  transfers between devices with their start and end apart: 5, of which 5 were waited for; matrix products, arithmetic and copies ran while one was open for 7% of the time, Pallas kernels for 0%

profile of v1, /device:TPU:0, one launch (start us, length us, event | category | flops | bytes accessed | tf_op | source)
XLA Modules:
  0.0 75.4 jit_solution(2160115678391193317)
XLA Ops:
  0.0 1.9 %copy-done = bf16[2048,768]{1,0:T(8,128)(2,1)S(1)} copy-done((bf16[2048,768]{1,0:T(8,128)(2,1)S(1)}, bf16[2048,768]{1,0:T(8,128)(2,1)}, u32[]{:S(2)}) %copy-start) | copy-done | bytes 3145752
  1.9 2.2 %convolution_convert_fusion.4 = bf16[256,768]{1,0:T(8,128)(2,1)S(1)} fusion(bf16[2048,256]{1,0:T(8,128)(2,1)} %param.7, bf16[2048,768]{1,0:T(8,128)(2,1)S(1)} %copy-done), kind=kOutput, calls=%fused_computation.15 | convolution fusion | flops 805502976 | bytes 4587520 | tf_op jit(solution)/shard_map/dot_general | solution.py:27
  4.1 0.6 collective-permute-start
  4.7 0.3 fusion.24
  5.0 1.0 %collective-permute-done = bf16[256,768]{1,0:T(8,128)(2,1)S(1)} collective-permute-done((bf16[256,768]{1,0:T(8,128)(2,1)S(1)}, bf16[256,768]{1,0:T(8,128)(2,1)S(1)}, u32[]{:S(2)}, u32[]{:S(2)}) %collective-permute-start) | collective-permute-done | bytes 393248 | tf_op jit(solution)/shard_map/ppermute | solution.py:23
  6.0 0.3 fusion.1
  6.4 2.9 %collective-permute-start.1 = (bf16[256,768]{0,1:T(8,128)(2,1)S(1)}, bf16[256,768]{0,1:T(8,128)(2,1)S(1)}, u32[]{:S(2)}, u32[]{:S(2)}) collective-permute-start(bf16[256,768]{0,1:T(8,128)(2,1)S(1)} %bitcast.93), channel_id=1, source_target_pairs={{0,2},{2,0},{1,3},{3,1},{4,6},{6,4},{5,7},{7,5},{8,10},{10,8},{9,1... | collective-permute-start | bytes 1179656 | tf_op jit(solution)/shard_map/ppermute | solution.py:23
  9.6 9.1 %collective-permute-done.1 = bf16[256,768]{0,1:T(8,128)(2,1)S(1)} collective-permute-done((bf16[256,768]{0,1:T(8,128)(2,1)S(1)}, bf16[256,768]{0,1:T(8,128)(2,1)S(1)}, u32[]{:S(2)}, u32[]{:S(2)}) %collective-permute-start.1) | collective-permute-done | bytes 393248 | tf_op jit(solution)/shard_map/ppermute | solution.py:23
  18.7 0.3 fusion.2
  19.0 1.9 %collective-permute-start.2 = (bf16[256,768]{0,1:T(8,128)(2,1)S(1)}, bf16[256,768]{0,1:T(8,128)(2,1)S(1)}, u32[]{:S(2)}, u32[]{:S(2)}) collective-permute-start(bf16[256,768]{0,1:T(8,128)(2,1)S(1)} %bitcast.94), channel_id=1, source_target_pairs={{0,4},{4,0},{1,5},{5,1},{2,6},{6,2},{3,7},{7,3},{8,12},{12,8},{9,1... | collective-permute-start | bytes 1179656 | tf_op jit(solution)/shard_map/ppermute | solution.py:23
  20.9 0.3 fusion.18
  21.2 8.5 %collective-permute-done.2 = bf16[256,768]{0,1:T(8,128)(2,1)S(1)} collective-permute-done((bf16[256,768]{0,1:T(8,128)(2,1)S(1)}, bf16[256,768]{0,1:T(8,128)(2,1)S(1)}, u32[]{:S(2)}, u32[]{:S(2)}) %collective-permute-start.2) | collective-permute-done | bytes 393248 | tf_op jit(solution)/shard_map/ppermute | solution.py:23
  29.6 0.3 fusion.3
  29.9 2.6 %collective-permute-start.3 = (bf16[256,768]{0,1:T(8,128)(2,1)S(1)}, bf16[256,768]{0,1:T(8,128)(2,1)S(1)}, u32[]{:S(2)}, u32[]{:S(2)}) collective-permute-start(bf16[256,768]{0,1:T(8,128)(2,1)S(1)} %bitcast.95), channel_id=1, source_target_pairs={{0,8},{8,0},{1,9},{9,1},{2,10},{10,2},{3,11},{11,3},{4,12},{12,4},... | collective-permute-start | bytes 1179656 | tf_op jit(solution)/shard_map/ppermute | solution.py:23
  32.8 16.2 %collective-permute-done.3 = bf16[256,768]{0,1:T(8,128)(2,1)S(1)} collective-permute-done((bf16[256,768]{0,1:T(8,128)(2,1)S(1)}, bf16[256,768]{0,1:T(8,128)(2,1)S(1)}, u32[]{:S(2)}, u32[]{:S(2)}) %collective-permute-start.3) | collective-permute-done | bytes 393248 | tf_op jit(solution)/shard_map/ppermute | solution.py:23
  49.3 0.9 %pad_maximum_fusion = bf16[2,1,256,768]{2,3,1,0:T(8,128)(2,1)} fusion(bf16[1,1,256,768]{2,3,1,0:T(8,128)(2,1)S(1)} %fusion.6), kind=kLoop, calls=%fused_computation.18 | loop fusion | flops 393216 | bytes 1179648 | tf_op jit(solution)/shard_map/stack | solution.py:10
  50.3 4.3 %all-to-all-start = ((bf16[2,1,256,768]{2,3,1,0:T(8,128)(2,1)}), bf16[2,1,256,768]{2,3,1,0:T(8,128)(2,1)}, u32[]{:S(2)}, u32[]{:S(2)}) async-start(bf16[2,1,256,768]{2,3,1,0:T(8,128)(2,1)} %pad_maximum_fusion), calls=%async_computation | async-start | bytes 1572864 | tf_op jit(solution)/shard_map/all_to_all | solution.py:9
  54.6 1.9 %slice.42 = bf16[1,4,256,256]{3,2,1,0:T(8,128)(2,1)} slice(bf16[1,14,256,256]{3,2,1,0:T(8,128)(2,1)} %param.10), slice={[0:1], [2:6], [0:256], [0:256]} | slice | bytes 1048576 | tf_op jit(solution)/shard_map/slice | solution.py:50
  56.5 2.3 %slice.43 = bf16[1,8,256,256]{3,2,1,0:T(8,128)(2,1)} slice(bf16[1,14,256,256]{3,2,1,0:T(8,128)(2,1)} %param.10), slice={[0:1], [6:14], [0:256], [0:256]} | slice | bytes 2097152 | tf_op jit(solution)/shard_map/slice | solution.py:50
  58.7 6.5 %all-to-all-done = bf16[2,1,256,768]{2,3,1,0:T(8,128)(2,1)} async-done(((bf16[2,1,256,768]{2,3,1,0:T(8,128)(2,1)}), bf16[2,1,256,768]{2,3,1,0:T(8,128)(2,1)}, u32[]{:S(2)}, u32[]{:S(2)}) %all-to-all-start) | async-done | bytes 786464 | tf_op jit(solution)/shard_map/all_to_all | solution.py:9
  65.2 1.6 %fusion.7 = bf16[768,256,1]{1,0,2:T(8,128)(2,1)S(1)} fusion(bf16[2,1,256,768]{2,3,1,0:T(8,128)(2,1)} %all-to-all-done, bf16[1,1,2,256,256]{4,3,2,1,0:T(8,128)(2,1)} %param.9), kind=kOutput, calls=%fused_computation.17 | convolution fusion | flops 201523200 | bytes 1441792 | tf_op jit(solution)/shard_map/hkl,hlr->kr/dot_general | solution.py:40
  66.8 3.1 %convolution_convert_fusion.2 = bf16[2,768,2,256]{3,1,2,0:T(8,128)(2,1)} fusion(bf16[2,2,256,256]{3,2,1,0:T(8,128)(2,1)} %bitcast.92, bf16[768,256,1]{1,0,2:T(8,128)(2,1)S(1)} %fusion.7, bf16[1,14,256,256]{3,2,1,0:T(8,128)(2,1)} %param.10), kind=kOutput, calls=%fused_computation.2 | convolution fusion | flops 605159424 | bytes 2752512 | tf_op jit(solution)/shard_map/jckl,jlr->jckr/dot_general | solution.py:51
  69.9 2.8 %convolution_convert_fusion.1 = bf16[4,768,2,256]{3,1,2,0:T(8,128)(2,1)S(1)} fusion(bf16[4,256,768,1]{1,2,3,0:T(8,128)(2,1)} %bitcast.90, bf16[4,2,256,256]{3,2,1,0:T(8,128)(2,1)} %bitcast.91), kind=kOutput, calls=%fused_computation.1 | convolution fusion | flops 806879232 | bytes 5767168 | tf_op jit(solution)/shard_map/jckl,jlr->jckr/dot_general | solution.py:51
  72.7 2.7 %convolution_convert_fusion = bf16[8,768,256]{1,2,0:T(8,128)(2,1)} fusion(bf16[8,256,768]{1,2,0:T(8,128)(2,1)S(1)} %bitcast.89, bf16[8,256,256]{2,1,0:T(8,128)(2,1)S(1)} %bitcast.96), kind=kOutput, calls=%fused_computation | convolution fusion | flops 806879232 | bytes 7340032 | tf_op jit(solution)/shard_map/ctk,ckr->ctr/dot_general | solution.py:55
  (8 shorter events, 0.9 us)
Async XLA Ops:
  0.0 1.9 %copy-start = (bf16[2048,768]{1,0:T(8,128)(2,1)S(1)}, bf16[2048,768]{1,0:T(8,128)(2,1)}, u32[]{:S(2)}) copy-start(bf16[2048,768]{1,0:T(8,128)(2,1)} %param.6) | copy-start | bytes 9437188
  0.0 4.7 %copy-start.2 = (bf16[1,4,2,256,256]{4,3,2,1,0:T(8,128)(2,1)S(1)}, bf16[1,4,2,256,256]{4,3,2,1,0:T(8,128)(2,1)}, u32[]{:S(2)}) copy-start(bf16[1,4,2,256,256]{4,3,2,1,0:T(8,128)(2,1)} %param.8) | copy-start | bytes 3145732
  4.1 1.9 %collective-permute-start = (bf16[256,768]{1,0:T(8,128)(2,1)S(1)}, bf16[256,768]{1,0:T(8,128)(2,1)S(1)}, u32[]{:S(2)}, u32[]{:S(2)}) collective-permute-start(bf16[256,768]{1,0:T(8,128)(2,1)S(1)} %convolution_convert_fusion.4), channel_id=1, source_target_pairs={{0,1},{1,0},{2,3},{3,2},{4,5},{5,4},{6,7},{7,6},{8,9},{9,8},{10,11... | collective-permute-start | bytes 1179656 | tf_op jit(solution)/shard_map/ppermute | solution.py:23
  6.4 12.3 %collective-permute-start.1 = (bf16[256,768]{0,1:T(8,128)(2,1)S(1)}, bf16[256,768]{0,1:T(8,128)(2,1)S(1)}, u32[]{:S(2)}, u32[]{:S(2)}) collective-permute-start(bf16[256,768]{0,1:T(8,128)(2,1)S(1)} %bitcast.93), channel_id=1, source_target_pairs={{0,2},{2,0},{1,3},{3,1},{4,6},{6,4},{5,7},{7,5},{8,10},{10,8},{9,1... | collective-permute-start | bytes 1179656 | tf_op jit(solution)/shard_map/ppermute | solution.py:23
  19.0 10.6 %collective-permute-start.2 = (bf16[256,768]{0,1:T(8,128)(2,1)S(1)}, bf16[256,768]{0,1:T(8,128)(2,1)S(1)}, u32[]{:S(2)}, u32[]{:S(2)}) collective-permute-start(bf16[256,768]{0,1:T(8,128)(2,1)S(1)} %bitcast.94), channel_id=1, source_target_pairs={{0,4},{4,0},{1,5},{5,1},{2,6},{6,2},{3,7},{7,3},{8,12},{12,8},{9,1... | collective-permute-start | bytes 1179656 | tf_op jit(solution)/shard_map/ppermute | solution.py:23
  29.9 19.1 %collective-permute-start.3 = (bf16[256,768]{0,1:T(8,128)(2,1)S(1)}, bf16[256,768]{0,1:T(8,128)(2,1)S(1)}, u32[]{:S(2)}, u32[]{:S(2)}) collective-permute-start(bf16[256,768]{0,1:T(8,128)(2,1)S(1)} %bitcast.95), channel_id=1, source_target_pairs={{0,8},{8,0},{1,9},{9,1},{2,10},{10,2},{3,11},{11,3},{4,12},{12,4},... | collective-permute-start | bytes 1179656 | tf_op jit(solution)/shard_map/ppermute | solution.py:23
  50.3 14.9 %all-to-all-start = ((bf16[2,1,256,768]{2,3,1,0:T(8,128)(2,1)}), bf16[2,1,256,768]{2,3,1,0:T(8,128)(2,1)}, u32[]{:S(2)}, u32[]{:S(2)}) async-start(bf16[2,1,256,768]{2,3,1,0:T(8,128)(2,1)} %pad_maximum_fusion), calls=%async_computation | async-start | bytes 1572864 | tf_op jit(solution)/shard_map/all_to_all | solution.py:9
  69.9 2.8 %copy-start.1 = (bf16[2048,256]{1,0:T(8,128)(2,1)S(1)}, bf16[2048,256]{1,0:T(8,128)(2,1)}, u32[]{:S(2)}) copy-start(bf16[2048,256]{1,0:T(8,128)(2,1)} %param.11) | copy-start | bytes 3145732
